TPU v7x, 32 devices: a whole 2x2x4 slice. The times are simulated.
32 devices in a mesh: section: 16 (over z, x, core), chan: 2 (over y).
Axes of the slice: x: 2, y: 2, z: 4, core: 2. Of those that a mesh axis runs over, the one named last changes fastest.
Arguments:
- voltages: bfloat16 [128, 2048, 2048], P('section', 'chan'), may hold values from -6 to 6
- fir_taps: float32 [4, 2048], replicated, may hold values from -1 to 1
- steer: float32 [32, 2048], replicated, may hold values from -0.05 to 0.05
- beam_dir: int32 [1024], replicated, may hold values from 0 to 31
- input_order: int32 [2048], replicated, may hold values from 0 to 2047, each once
Outputs:
- vis: bfloat16 [32, 2048, 2048], P(('section', 'chan'))
- beams: bfloat16 [32, 2, 1024, 128], P(('section', 'chan'))
Inputs may be any that keep to these rules, and one draw needn't show every extreme that they name: `input_order`: each of 0 to 2047 once.
All inputs are finite; a program needn't handle non-finite values.
Results may differ from a plain program's by a relative error of at most 0.0058.
Values may be sent and summed in bfloat16 or wider, within the bound.
No kernel may reach another device: no remote copies, remote signals or barrier semaphores. Data moves between devices by JAX's collectives and lax.ppermute only.
A program may use at most 192 MiB of HBM per device.

v0:
```python
import math

import jax
import jax.numpy as jnp
from jax import lax
from jax.sharding import PartitionSpec as P

CH_DEV = 1


def shifted(block, axis, distance):
    devices = range(lax.axis_size(axis))
    route = [(i - distance, i) for i in devices if i - distance in devices]
    return lax.ppermute(block, axis, route)


def fourier_table(frame, first, channels):
    samples = lax.broadcasted_iota(jnp.int32, (channels, frame), 1)
    bins = lax.broadcasted_iota(jnp.int32, (channels, frame), 0) + first
    turns = bins * samples % frame
    angle = turns.astype(jnp.float32) * (2.0 * math.pi / frame)
    factor = 1.0 / math.sqrt(frame)
    return jnp.stack([jnp.cos(angle) * factor, -jnp.sin(angle) * factor], axis=1).reshape(
        2 * channels, frame
    )


def filter_frames(fir_taps, extended, lag, spec_dev):
    filtered = jnp.zeros((spec_dev, extended.shape[1], extended.shape[2]), jnp.float32)
    for tap_index in range(lag + 1):
        offset = lag - tap_index
        filtered = filtered + fir_taps[tap_index][None, None, :] * extended[
            offset : offset + spec_dev
        ].astype(jnp.float32)
    return filtered


def on_device(voltages, fir_taps, steer, beam_dir, input_order):
    section_count = lax.axis_size("section")
    chan_count = lax.axis_size("chan")
    spec_dev = voltages.shape[0]
    inputs_here = voltages.shape[1]
    frame = voltages.shape[2]
    lag = fir_taps.shape[0] - 1
    channels = CH_DEV * section_count * chan_count
    first = frame // 8
    table = fourier_table(frame, first, channels)

    def transform(signal):
        return jnp.einsum("kn,sin->ksi", table, signal, precision=lax.Precision.HIGH)

    extended = jnp.concatenate(
        [jnp.zeros((lag, inputs_here, frame), voltages.dtype), voltages], axis=0
    )
    spectra = transform(filter_frames(fir_taps, extended, lag, spec_dev))
    tail_rows = []
    for lead in range(lag):
        partial_sum = jnp.zeros((inputs_here, frame), jnp.float32)
        for tap_index in range(lead + 1, lag + 1):
            partial_sum = partial_sum + fir_taps[tap_index][None, :] * voltages[
                spec_dev + lead - tap_index
            ].astype(jnp.float32)
        tail_rows.append(partial_sum)
    tail_terms = transform(jnp.stack(tail_rows, axis=0))
    carried = shifted(tail_terms, "section", 1)
    spectra = spectra.at[:, :lag, :].add(carried)
    grouped = spectra.astype(jnp.bfloat16).reshape(
        section_count, chan_count * CH_DEV, 2, spec_dev, inputs_here
    )
    across = lax.all_to_all(grouped, "chan", split_axis=1, concat_axis=4, tiled=True)
    regrouped = lax.all_to_all(across, "section", split_axis=0, concat_axis=3, tiled=True)
    total_frames = regrouped.shape[3]
    total_inputs = regrouped.shape[4]
    column_ids = lax.broadcasted_iota(jnp.int32, (total_inputs, total_inputs), 1)
    selector = (column_ids == input_order[:, None]).astype(jnp.bfloat16)
    vis_scale = 1.0 / math.sqrt(total_frames)
    block_rows = min(512, total_inputs)
    device_index = lax.axis_index("section") * chan_count + lax.axis_index("chan")
    contract = (((1,), (1,)), ((), ()))
    flat = regrouped[0, 0].reshape(2 * total_frames, total_inputs)
    ordered = lax.dot_general(selector, flat, contract, preferred_element_type=jnp.float32).astype(
        jnp.bfloat16
    )
    real_part = ordered[:, :total_frames]
    imag_part = ordered[:, total_frames:]
    rotated = jnp.concatenate([-imag_part, real_part], axis=1)
    both_sides = jnp.concatenate([ordered, rotated], axis=0)
    vis_blocks = []
    for row_start in range(0, total_inputs, block_rows):
        products = lax.dot_general(
            ordered[row_start : row_start + block_rows],
            both_sides,
            contract,
            preferred_element_type=jnp.float32,
        )
        row_index = lax.broadcasted_iota(jnp.int32, (block_rows, total_inputs), 0) + row_start
        col_index = lax.broadcasted_iota(jnp.int32, (block_rows, total_inputs), 1)
        chosen = jnp.where(
            col_index >= row_index, products[:, :total_inputs], products[:, total_inputs:]
        )
        vis_blocks.append((chosen * vis_scale).astype(jnp.bfloat16))
    vis_list = [jnp.concatenate(vis_blocks, axis=0)]
    global_channel = device_index * CH_DEV + 0
    frequency = (first + global_channel).astype(jnp.float32)
    phase = jnp.take(steer, beam_dir, axis=0) * frequency
    w_real = (jnp.cos(phase) / math.sqrt(total_inputs)).astype(jnp.bfloat16)
    w_imag = (-jnp.sin(phase) / math.sqrt(total_inputs)).astype(jnp.bfloat16)
    beam_count = w_real.shape[0]
    weights = jnp.concatenate([w_real, w_imag], axis=0)
    mixed = jnp.dot(weights, ordered, preferred_element_type=jnp.float32)
    from_real = mixed[:beam_count]
    from_imag = mixed[beam_count:]
    beam_real = from_real[:, :total_frames] - from_imag[:, total_frames:]
    beam_imag = from_real[:, total_frames:] + from_imag[:, :total_frames]
    beam_list = [jnp.stack([beam_real, beam_imag], axis=0).astype(jnp.bfloat16)]
    return (jnp.stack(vis_list, axis=0), jnp.stack(beam_list, axis=0))


def solution(mesh):
    return jax.shard_map(
        on_device,
        mesh=mesh,
        in_specs=(P("section", "chan", None), P(), P(), P(), P()),
        out_specs=(P(("section", "chan"), None, None), P(("section", "chan"), None, None, None)),
        check_vma=False,
    )
```

profile of v0, /device:TPU:0, one launch (start us, length us, event | category | flops | bytes accessed | tf_op | source)
XLA Modules:
  0.0 185.3 jit_solution(13955273857756714590)
XLA Ops:
  0.7 0.9 fusion.63
  1.6 1.1 cosine_multiply_fusion
  3.5 8.4 %fusion.24 = (f32[1,1024,2048]{2,1,0:T(8,128)S(1)}, f32[1,1024,2048]{2,1,0:T(8,128)S(1)}, f32[1,1024,2048]{2,1,0:T(8,128)}) fusion(bf16[8,1024,2048]{2,1,0:T(8,128)(2,1)} %param.7, f32[2048]{0:T(1024)S(1)} %bitcast.33, f32[2048]{0:T(1024)S(1)} %bitcast.35, f32[2048]{0:T(1024)S(1)} %bitcast.31), kind=kLoop, calls=%fused_computation.34 | loop fusion | flops 25165824 | bytes 37773312 | tf_op jit(solution)/shard_map/add | solution.py:60
  12.0 15.1 %fusion.16 = f32[64,3,1024]{2,0,1:T(8,128)} fusion(f32[64,2048,1]{1,0,2:T(8,128)S(1)} %reshape.227, f32[1,1024,2048]{2,1,0:T(8,128)} %get-tuple-element.16, f32[1,1024,2048]{2,1,0:T(8,128)S(1)} %get-tuple-element.15, f32[1,1024,2048]{2,1,0:T(8,128)S(1)} %get-tuple-element.14), kind=kOutput, calls=%fused_computation.20 | convolution fusion | flops 2428502016 | bytes 26476544 | tf_op jit(solution)/shard_map/kn,sin->ksi/dot_general | solution.py:50
  27.1 2.6 %collective-permute-start = (f32[64,3,1024]{2,0,1:T(8,128)}, f32[64,3,1024]{2,0,1:T(8,128)S(1)}, u32[]{:S(2)}, u32[]{:S(2)}) collective-permute-start(f32[64,3,1024]{2,0,1:T(8,128)} %fusion.16), channel_id=1, source_target_pairs={{0,2},{2,4},{4,6},{6,8},{8,10},{10,12},{12,14},{14,16},{16,18},{18... | collective-permute-start | bytes 2359304 | tf_op jit(solution)/shard_map/ppermute | solution.py:14
  29.7 57.4 %fusion = f32[64,8,1024]{2,0,1:T(8,128)S(1)} fusion(f32[64,2048,1]{1,0,2:T(8,128)S(1)} %reshape.227, bf16[8,1024,2048]{2,1,0:T(8,128)(2,1)} %param.7, f32[2048]{0:T(1024)S(1)} %bitcast.34, f32[2048]{0:T(1024)S(1)} %bitcast.36, f32[2048]{0:T(1024)S(1)} %bitcast.32, f32[2048]{0:T(1024)S(1)} %bitcast.37), kind=kOutput, calls=%fused_computation.1 | convolution fusion | flops 6627000320 | bytes 36208640 | tf_op jit(solution)/shard_map/kn,sin->ksi/dot_general | solution.py:50
  87.5 0.4 reshape.217
  87.9 0.9 copy.18
  88.8 17.8 %all_to_all.33 = bf16[16,2,2,8,1024]{4,3,2,0,1:T(8,128)(2,1)S(1)} all-to-all(bf16[16,2,2,8,1024]{4,3,2,0,1:T(8,128)(2,1)S(1)} %copy.18), channel_id=1, replica_groups=mesh['section'=16,'chan'=2] {'chan'}, dimensions={1} | all-to-all | bytes 2097152 | tf_op jit(solution)/shard_map/all_to_all | solution.py:70
  106.6 1.1 copy.22
  107.8 5.3 %all-to-all-start.1 = ((bf16[16,1,2,8,2048]{4,3,2,1,0:T(8,128)(2,1)}), bf16[16,1,2,8,2048]{4,3,2,1,0:T(8,128)(2,1)S(1)}, u32[]{:S(2)}, u32[]{:S(2)}) async-start(bf16[16,1,2,8,2048]{4,3,2,1,0:T(8,128)(2,1)} %bitcast.6), calls=%async_computation.1 | async-start | bytes 2097152 | tf_op jit(solution)/shard_map/all_to_all | solution.py:71
  113.1 6.7 %gather_fusion = f32[1024,2048]{1,0:T(8,128)} fusion(f32[32,2048]{1,0:T(8,128)S(1)} %copy-done, s32[1024]{0:T(1024)S(1)} %fusion.59), kind=kCustom, calls=%fused_computation | custom fusion | bytes 16781312 | tf_op jit(solution)/shard_map/jit(_take)/gather | solution.py:105
  119.8 35.1 %multiply_convert_fusion.1 = (bf16[1024,2048]{1,0:T(8,128)(2,1)}, bf16[1024,2048]{1,0:T(8,128)(2,1)}) fusion(f32[1024,2048]{1,0:T(8,128)} %gather_fusion, f32[]{:T(128)S(6)} %convert_element_type.96, pred[1024]{0:T(1024)(128)(4,1)S(1)} %compare_and_fusion), kind=kLoop, calls=%fused_computation.42 | loop fusion | flops 14680064 | bytes 16778244 | tf_op jit(solution)/shard_map/convert_element_type | solution.py:106
  155.0 3.1 %fusion.39 = bf16[2048,256]{1,0:T(8,128)(2,1)S(1)} fusion(bf16[256,2048]{1,0:T(8,128)(2,1)S(1)} %bitcast.30, s32[2048]{0:T(1024)S(1)} %copy-done.4), kind=kOutput, calls=%fused_computation.61 | convolution fusion | flops 2152202240 | bytes 2105344 | tf_op jit(solution)/shard_map/dot_general | solution.py:81
  158.3 1.3 fusion.54
  159.6 4.7 %fusion.52 = f32[512,4096]{1,0:T(8,128)} fusion(bf16[2048,256]{1,0:T(8,128)(2,1)S(1)} %fusion.39, bf16[2048,128]{1,0:T(8,128)(2,1)S(1)} %get-tuple-element.22, bf16[2048,128]{1,0:T(8,128)(2,1)S(1)} %get-tuple-element.21), kind=kOutput, calls=%fused_computation.84 | convolution fusion | flops 1080033280 | bytes 10747904 | tf_op jit(solution)/shard_map/dot_general | solution.py:90
  164.3 1.3 fusion.50
  165.6 1.3 fusion.48
  167.0 5.9 %fusion.26 = f32[2048,256]{1,0:T(8,128)} fusion(bf16[2048,256]{1,0:T(8,128)(2,1)S(1)} %fusion.39, bf16[1024,2048]{1,0:T(8,128)(2,1)} %get-tuple-element.18, bf16[1024,2048]{1,0:T(8,128)(2,1)S(1)} %copy-done.2), kind=kOutput, calls=%fused_computation.37 | convolution fusion | flops 2164260864 | bytes 11534336 | tf_op jit(solution)/shard_map/dot_general | solution.py:110
  172.9 1.6 fusion.46
  174.5 0.8 pad_maximum_fusion.1
  175.3 4.7 %fusion.36 = (bf16[512,2048]{1,0:T(8,128)(2,1)S(1)}, bf16[512,2048]{1,0:T(8,128)(2,1)S(1)}) fusion(f32[512,4096]{1,0:T(8,128)} %fusion.52, s32[512]{0:T(512)S(1)} %iota_add_fusion.2, f32[512,4096]{1,0:T(8,128)S(1)} %fusion.54), kind=kLoop, calls=%fused_computation.53 | loop fusion | flops 8388608 | bytes 20973568 | tf_op jit(solution)/shard_map/convert_element_type | solution.py:101
  180.1 1.2 fusion.32
  181.3 4.0 %maximum_bitcast_fusion = bf16[1,2048,2048]{2,1,0:T(8,128)(2,1)} fusion(bf16[512,2048]{1,0:T(8,128)(2,1)S(1)} %get-tuple-element.29, bf16[512,2048]{1,0:T(8,128)(2,1)S(1)} %get-tuple-element.30, bf16[512,2048]{1,0:T(8,128)(2,1)S(1)} %get-tuple-element.31, bf16[512,2048]{1,0:T(8,128)(2,1)S(1)} %get-tuple-element.32), kind=kLoop, calls=%fused_computation.36 | loop fusion | flops 33554432 | bytes 16777216 | tf_op jit(solution)/shard_map/stack | solution.py:116
  (25 shorter events, 1.5 us)
Async XLA Ops:
  0.6 112.5 %copy-start = (f32[32,2048]{1,0:T(8,128)S(1)}, f32[32,2048]{1,0:T(8,128)}, u32[]{:S(2)}) copy-start(f32[32,2048]{1,0:T(8,128)} %param.9) | copy-start | bytes 786436
  27.1 60.0 %collective-permute-start = (f32[64,3,1024]{2,0,1:T(8,128)}, f32[64,3,1024]{2,0,1:T(8,128)S(1)}, u32[]{:S(2)}, u32[]{:S(2)}) collective-permute-start(f32[64,3,1024]{2,0,1:T(8,128)} %fusion.16), channel_id=1, source_target_pairs={{0,2},{2,4},{4,6},{6,8},{8,10},{10,12},{12,14},{14,16},{16,18},{18... | collective-permute-start | bytes 2359304 | tf_op jit(solution)/shard_map/ppermute | solution.py:14
  87.1 26.0 %copy-start.3 = (s32[1024]{0:T(1024)S(1)}, s32[1024]{0:T(1024)}, u32[]{:S(2)}) copy-start(s32[1024]{0:T(1024)} %param.10) | copy-start | bytes 12292
  107.8 47.1 %all-to-all-start.1 = ((bf16[16,1,2,8,2048]{4,3,2,1,0:T(8,128)(2,1)}), bf16[16,1,2,8,2048]{4,3,2,1,0:T(8,128)(2,1)S(1)}, u32[]{:S(2)}, u32[]{:S(2)}) async-start(bf16[16,1,2,8,2048]{4,3,2,1,0:T(8,128)(2,1)} %bitcast.6), calls=%async_computation.1 | async-start | bytes 2097152 | tf_op jit(solution)/shard_map/all_to_all | solution.py:71
  119.8 35.2 %copy-start.4 = (s32[2048]{0:T(1024)S(1)}, s32[2048]{0:T(1024)}, u32[]{:S(2)}) copy-start(s32[2048]{0:T(1024)} %param.11) | copy-start | bytes 24580
  164.3 2.6 %copy-start.2 = (bf16[1024,2048]{1,0:T(8,128)(2,1)S(1)}, bf16[1024,2048]{1,0:T(8,128)(2,1)}, u32[]{:S(2)}) copy-start(bf16[1024,2048]{1,0:T(8,128)(2,1)} %get-tuple-element.17) | copy-start | bytes 12582916
  181.3 4.0 %copy-start.1 = (f32[32,2048]{1,0:T(8,128)S(1)}, f32[32,2048]{1,0:T(8,128)}, u32[]{:S(2)}) copy-start(f32[32,2048]{1,0:T(8,128)} %param.9) | copy-start | bytes 786436
where the time goes:
time: 186 us; the launch traced here: 185 us
  matrix products  90.2 us (48%)
  other arithmetic  57.6 us (31%)
  blocking collectives  17.8 us (10%)
  local copies, waits for them, and re-layouts  11 us (6%)
  starting transfers between devices  7.84 us (4%)
    dot_general x2, matrix products, transform(): jnp.einsum('kn,sin->ksi', table, signal, precision=lax.Precision.HIGH)  72.5 us
    convert_element_type x1, other arithmetic, on_device(): w_real = (jnp.cos(phase) / math.sqrt(total_inputs)).astype(jnp.bfloat16)  35.1 us
    all_to_all x1, blocking collectives, on_device(): lax.all_to_all(grouped, 'chan', split_axis=1, concat_axis=4, tiled=True)  17.8 us
    dot_general x4, matrix products, on_device(): lax.dot_general(ordered[row_start:row_start + block_rows], both_sides, co...  8.64 us
    add x1, other arithmetic, on_device(): partial_sum + fir_taps[tap_index][None, :] * voltages[spec_dev + lead - t...  8.44 us
    gather x1, local copies, waits for them, and re-layouts, on_device(): phase = jnp.take(steer, beam_dir, axis=0) * frequency  6.68 us
    convert_element_type x2, other arithmetic, on_device(): vis_blocks.append((chosen * vis_scale).astype(jnp.bfloat16))  5.97 us
    dot_general x1, matrix products, on_device(): mixed = jnp.dot(weights, ordered, preferred_element_type=jnp.float32)  5.92 us
  transfers between devices with their start and end apart: 2, of which 0 were waited for; matrix products, arithmetic and copies ran while one was open for 54% of the time, Pallas kernels for 0%

commit v1 on v0

v1 whole, which is shorter than its diff:
```python
import functools
import math

import jax
import jax.numpy as jnp
import numpy as np
from jax import lax
from jax.experimental import pallas as pl
from jax.experimental.pallas import tpu as pltpu
from jax.sharding import PartitionSpec as P

MINOR = (((1,), (1,)), ((), ()))
MAJOR = (((0,), (0,)), ((), ()))
VMEM_BYTES = 56 << 20
LANES = 128


def fourier_table(frame, first, channels):
    turns = np.arange(first, first + channels)[:, None] * np.arange(frame)[None, :] % frame
    angle = turns * (2.0 * math.pi / frame)
    factor = 1.0 / math.sqrt(frame)
    pair = np.stack([np.cos(angle) * factor, -np.sin(angle) * factor], axis=1)
    return pair.reshape(2 * channels, frame).astype(np.float32)


def frame_products(frames, taps, volts_ref, wave_ref, fir_ref, held, table, sems, block, emit):
    rows = wave_ref.shape[0]
    blocks = volts_ref.shape[1] // block
    count = len(frames)

    def copy(b, k):
        start = pl.multiple_of(b * block, block)
        return pltpu.make_async_copy(
            volts_ref.at[frames[k], pl.ds(start, block)],
            held.at[b * count + k],
            sems.at[b * count + k],
        )

    for b in range(blocks):
        for k in range(count):
            copy(b, k).start()
    for m in range(taps):
        table[m * rows : (m + 1) * rows, :] = (wave_ref[...] * fir_ref[m : m + 1, :]).astype(
            table.dtype
        )

    def body(b, carry):
        sums = {}
        for k in range(count):
            copy(b, k).wait()
            terms = lax.dot_general(
                table[...], held[b * count + k], MINOR, preferred_element_type=jnp.float32
            )
            for m in range(taps):
                part = terms[m * rows : (m + 1) * rows]
                at = frames[k] + m
                sums[at] = sums[at] + part if at in sums else part
        emit(pl.ds(pl.multiple_of(b * block, block), block), sums)
        return carry

    lax.fori_loop(0, blocks, body, 0)


def last_frames_kernel(
    total, taps, block, volts_ref, wave_ref, fir_ref, own_ref, tail_ref, held, table, sems
):
    lag = taps - 1

    def emit(at, sums):
        for k in range(lag):
            own_ref[k, :, at] = sums[total - lag + k]
            tail_ref[k, :, at] = sums[total + k].astype(tail_ref.dtype)

    frames = list(range(total - lag, total))
    frame_products(frames, taps, volts_ref, wave_ref, fir_ref, held, table, sems, block, emit)


def first_frames_kernel(
    total, taps, block, volts_ref, wave_ref, fir_ref, own_ref, sum_ref, held, table, sems
):
    lag = taps - 1

    def emit(at, sums):
        for t in range(total):
            value = sums[t]
            if t >= total - lag:
                value = value + own_ref[t - (total - lag), :, at]
            sum_ref[t, :, at] = value

    frames = list(range(total - lag))
    frame_products(frames, taps, volts_ref, wave_ref, fir_ref, held, table, sems, block, emit)


def join_kernel(sum_ref, carried_ref, out_ref, rows):
    total, count = sum_ref.shape[0], sum_ref.shape[1]
    lag = carried_ref.shape[0]
    for t in range(total):
        value = sum_ref[t]
        if t < lag:
            value = value + carried_ref[t].astype(jnp.float32)
        for j in range(rows.shape[0]):
            rows[j, pl.ds(t, count, stride=total), :] = value[:, j * LANES : (j + 1) * LANES]
    for j in range(rows.shape[0]):
        out_ref[:, j * LANES : (j + 1) * LANES] = rows[j].astype(out_ref.dtype)


def channel_kernel(
    scale, got_ref, order_ref, weight_ref, dir_ref, vis_ref, beam_ref, flat, mixed, turned
):
    sections, chans, pair, inputs = got_ref.shape
    frames = sections * pair // 2
    total = flat.shape[1]
    block = vis_ref.shape[0]
    step = pl.program_id(0)

    @pl.when(step == 0)
    def _():
        for c in range(chans):
            flat[:, c * inputs : (c + 1) * inputs] = got_ref[:, c].reshape(2 * frames, inputs)
        for start in range(0, total, block):
            source = lax.broadcasted_iota(jnp.int32, (total, block), 0)
            chosen = (source == order_ref[:, start : start + block]).astype(jnp.bfloat16)
            picked = jnp.dot(flat[...], chosen, preferred_element_type=jnp.float32)
            parts = picked.reshape(sections, 2, pair // 2, block)
            real = parts[:, 0].reshape(frames, block)
            imag = parts[:, 1].reshape(frames, block)
            mixed[:, start : start + block] = jnp.concatenate([real, imag], axis=0).astype(
                mixed.dtype
            )
            turned[:, start : start + block] = jnp.concatenate([-imag, real], axis=0).astype(
                turned.dtype
            )
        both = lax.dot_general(
            weight_ref[...], mixed[...], MINOR, preferred_element_type=jnp.float32
        )
        dirs = both.shape[0] // 2
        beam_real = both[:dirs, :frames] - both[dirs:, frames:]
        beam_imag = both[:dirs, frames:] + both[dirs:, :frames]
        formed = jnp.concatenate([beam_real, beam_imag], axis=1).astype(jnp.bfloat16)
        beams = beam_ref.shape[1]
        row = lax.broadcasted_iota(jnp.int32, (dirs, beams), 0)
        chosen = (row == dir_ref[...]).astype(jnp.bfloat16)
        spread = lax.dot_general(chosen, formed, MAJOR, preferred_element_type=jnp.float32)
        beam_ref[0] = spread[:, :frames].astype(beam_ref.dtype)
        beam_ref[1] = spread[:, frames:].astype(beam_ref.dtype)

    here = pl.ds(pl.multiple_of(step * block, block), block)
    left = mixed[:, here]
    products = lax.dot_general(left, mixed[...], MAJOR, preferred_element_type=jnp.float32)
    vis_ref[...] = (products * scale).astype(vis_ref.dtype)
    other = turned[:, here]
    real = lax.dot_general(left, left, MAJOR, preferred_element_type=jnp.float32)
    imag = lax.dot_general(left, other, MAJOR, preferred_element_type=jnp.float32)
    row = lax.broadcasted_iota(jnp.int32, (block, block), 0)
    col = lax.broadcasted_iota(jnp.int32, (block, block), 1)
    vis_ref[:, here] = (jnp.where(col >= row, real, imag) * scale).astype(vis_ref.dtype)
    mixed[:, here] = other


def on_device(voltages, fir_taps, steer, beam_dir, input_order):
    section_count = lax.axis_size("section")
    chan_count = lax.axis_size("chan")
    devices = section_count * chan_count
    spec_dev, inputs_here, frame = voltages.shape
    taps = fir_taps.shape[0]
    lag = taps - 1
    channels = devices
    first = frame // 8
    rows = 2 * channels
    total_inputs = inputs_here * chan_count
    total_frames = spec_dev * section_count
    wave = jnp.asarray(fourier_table(frame, first, channels))
    block = min(256, inputs_here)
    blocks = inputs_here // block
    whole = pl.BlockSpec(memory_space=pltpu.VMEM)

    def call(kernel, frames, extra, outs):
        return pl.pallas_call(
            functools.partial(kernel, spec_dev, taps, block),
            in_specs=[pl.BlockSpec(memory_space=pl.ANY)] + [whole] * (2 + len(extra)),
            out_specs=[whole] * len(outs),
            out_shape=outs,
            scratch_shapes=[
                pltpu.VMEM((frames * blocks, block, frame), voltages.dtype),
                pltpu.VMEM((taps * rows, frame), jnp.bfloat16),
                pltpu.SemaphoreType.DMA((frames * blocks,)),
            ],
            compiler_params=pltpu.CompilerParams(vmem_limit_bytes=VMEM_BYTES),
            cost_estimate=pl.CostEstimate(
                flops=2 * taps * rows * frame * inputs_here * frames,
                bytes_accessed=2 * frame * inputs_here * frames,
                transcendentals=0,
            ),
        )(voltages, wave, fir_taps, *extra)

    own, tail = call(
        last_frames_kernel,
        lag,
        (),
        [
            jax.ShapeDtypeStruct((lag, rows, inputs_here), jnp.float32),
            jax.ShapeDtypeStruct((lag, rows, inputs_here), jnp.bfloat16),
        ],
    )
    carried = lax.ppermute(tail, "section", [(i, i + 1) for i in range(section_count - 1)])
    (sums,) = call(
        first_frames_kernel,
        spec_dev - lag,
        (own,),
        [jax.ShapeDtypeStruct((spec_dev, rows, inputs_here), jnp.float32)],
    )
    spectra = pl.pallas_call(
        join_kernel,
        in_specs=[whole] * 2,
        out_specs=whole,
        out_shape=jax.ShapeDtypeStruct((rows * spec_dev, inputs_here), jnp.bfloat16),
        scratch_shapes=[pltpu.VMEM((inputs_here // LANES, rows * spec_dev, LANES), jnp.float32)],
        compiler_params=pltpu.CompilerParams(vmem_limit_bytes=VMEM_BYTES),
    )(sums, carried)
    got = lax.all_to_all(
        spectra.reshape(devices, 2 * spec_dev, inputs_here),
        ("section", "chan"),
        split_axis=0,
        concat_axis=0,
        tiled=True,
    ).reshape(section_count, chan_count, 2 * spec_dev, inputs_here)

    channel = lax.axis_index("section") * chan_count + lax.axis_index("chan")
    phase = steer * (first + channel).astype(jnp.float32)
    size = math.sqrt(total_inputs)
    weights = jnp.concatenate([jnp.cos(phase) / size, -jnp.sin(phase) / size], axis=0).astype(
        jnp.bfloat16
    )
    beam_count = beam_dir.shape[0]
    vis_rows = min(256, total_inputs)
    fixed = lambda shape: pl.BlockSpec(shape, lambda i: (0,) * len(shape))
    vis, beams = pl.pallas_call(
        functools.partial(channel_kernel, 1.0 / math.sqrt(total_frames)),
        grid=(total_inputs // vis_rows,),
        in_specs=[
            fixed(got.shape),
            fixed((1, total_inputs)),
            fixed(weights.shape),
            fixed((1, beam_count)),
        ],
        out_specs=[
            pl.BlockSpec((vis_rows, total_inputs), lambda i: (i, 0)),
            fixed((2, beam_count, total_frames)),
        ],
        out_shape=[
            jax.ShapeDtypeStruct((total_inputs, total_inputs), jnp.bfloat16),
            jax.ShapeDtypeStruct((2, beam_count, total_frames), jnp.bfloat16),
        ],
        scratch_shapes=[
            pltpu.VMEM((2 * total_frames, total_inputs), jnp.bfloat16),
            pltpu.VMEM((2 * total_frames, total_inputs), jnp.bfloat16),
            pltpu.VMEM((2 * total_frames, total_inputs), jnp.bfloat16),
        ],
        compiler_params=pltpu.CompilerParams(vmem_limit_bytes=VMEM_BYTES),
    )(got, input_order.reshape(1, total_inputs), weights, beam_dir.reshape(1, beam_count))
    return (vis[None], beams[None])


def solution(mesh):
    return jax.shard_map(
        on_device,
        mesh=mesh,
        in_specs=(P("section", "chan", None), P(), P(), P(), P()),
        out_specs=(P(("section", "chan"), None, None), P(("section", "chan"), None, None, None)),
        check_vma=False,
    )
```

time: 186 us -> 80.8 us (0.43)
  matrix products: 90.2 us -> 0 us
  other arithmetic: 57.6 us -> 1.73 us
  Pallas kernels: 0 us -> 42.4 us
  waiting for transfers between devices: 0.01 us -> 24.5 us
  blocking collectives: 17.8 us -> 0 us
  local copies, waits for them, and re-layouts: 11 us -> 1.71 us
    dot_general x8 -> x0, matrix products: 90.2 us -> none  [the longest x2 72.5 us: transform(): jnp.einsum('kn,sin->ksi', table, signal, precision=lax.Precision.HIGH)]
    pallas_call x0 -> x4, Pallas kernels: none -> 42.4 us  [the longest x2 27.8 us: call(): pl.pallas_call(functools.partial(kernel, spec_dev, taps, block), in_specs...]
    convert_element_type x4 -> x0, other arithmetic: 41.2 us -> none  [the longest x1 35.1 us: on_device(): w_real = (jnp.cos(phase) / math.sqrt(total_inputs)).astype(jnp.bfloat16)]
    all_to_all x1, waiting for transfers between devices: 0.01 us -> 24.5 us  [on_device(): lax.all_to_all(spectra.reshape(devices, 2 * spec_dev, inputs_here), ('sec...]
    all_to_all x1 -> x0, blocking collectives: 17.8 us -> none  [on_device(): lax.all_to_all(grouped, 'chan', split_axis=1, concat_axis=4, tiled=True)]
    add x5 -> x0, other arithmetic: 8.46 us -> none  [the longest x1 8.44 us: on_device(): partial_sum + fir_taps[tap_index][None, :] * voltages[spec_dev + lead - t...]
    gather x1 -> x0, local copies, waits for them, and re-layouts: 6.68 us -> none  [on_device(): phase = jnp.take(steer, beam_dir, axis=0) * frequency]
    another operation x4 -> x1, other arithmetic: 6.48 us -> 0.99 us  [the longest x1 3.98 us: on_device(): return (jnp.stack(vis_list, axis=0), jnp.stack(beam_list, axis=0))]
  transfers between devices with their start and end apart: 2 -> 2, of which waited for: 0 -> 1; matrix products, arithmetic and copies ran while one was open for 54% -> 2% of each run, Pallas kernels for 0% -> 21%
where the time goes in v1:
time: 80.8 us; the launch traced here: 80.5 us
  Pallas kernels  42.4 us (52%)
  waiting for transfers between devices  24.5 us (30%)
  starting transfers between devices  9.5 us (12%)
  other arithmetic  1.73 us (2%)
  local copies, waits for them, and re-layouts  1.71 us (2%)
    pallas_call x2, Pallas kernels, call(): pl.pallas_call(functools.partial(kernel, spec_dev, taps, block), in_specs...  27.8 us
    all_to_all x1, waiting for transfers between devices, on_device(): lax.all_to_all(spectra.reshape(devices, 2 * spec_dev, inputs_here), ('sec...  24.5 us
    pallas_call x1, Pallas kernels, on_device(): pl.pallas_call(functools.partial(channel_kernel, 1.0 / math.sqrt(total_fr...  11.1 us
    all_to_all x1, starting transfers between devices, on_device(): lax.all_to_all(spectra.reshape(devices, 2 * spec_dev, inputs_here), ('sec...  7.12 us
    pallas_call x1, Pallas kernels, on_device(): pl.pallas_call(join_kernel, in_specs=[whole] * 2, out_specs=whole, out_sh...  3.45 us
    ppermute x1, starting transfers between devices, on_device(): lax.ppermute(tail, 'section', [(i, i + 1) for i in range(section_count -...  2.38 us
    unnamed x6, local copies, waits for them, and re-layouts  1.71 us
  transfers between devices with their start and end apart: 2, of which 1 were waited for; matrix products, arithmetic and copies ran while one was open for 2% of the time, Pallas kernels for 21%

profile of v1, /device:TPU:0, one launch (start us, length us, event | category | flops | bytes accessed | tf_op | source)
XLA Modules:
  0.0 80.5 jit_solution(7296293303756363355)
XLA Ops:
  0.6 10.8 %shard_map.77 = (f32[3,64,1024]{2,1,0:T(8,128)}, bf16[3,64,1024]{2,1,0:T(8,128)(2,1)}) custom-call(bf16[8,1024,2048]{2,1,0:T(8,128)(2,1)} %volts_ref.3, f32[64,2048]{1,0:T(8,128)} %constant.18.clone.wave_ref, f32[4,2048]{1,0:T(4,128)} %fir_ref.3), custom_call_target="tpu_custom_call" | custom-call | flops 3221225472 | bytes 12582912 | tf_op jit(solution)/shard_map/pallas_call | solution.py:178
  11.4 2.4 %collective-permute-start = (bf16[3,64,1024]{2,1,0:T(8,128)(2,1)}, bf16[3,64,1024]{2,1,0:T(8,128)(2,1)S(1)}, u32[]{:S(2)}, u32[]{:S(2)}) collective-permute-start(bf16[3,64,1024]{2,1,0:T(8,128)(2,1)} %get-tuple-element.7), channel_id=1, source_target_pairs={{0,2},{2,4},{4,6},{6,8},{8,10},{10,12},{12,14},{14,16},{16,18},{18... | collective-permute-start | bytes 1179656 | tf_op jit(solution)/shard_map/ppermute | solution.py:205
  13.8 0.0 copy-start.2
  13.8 17.0 %shard_map.78.sum_ref = f32[8,64,1024]{2,1,0:T(8,128)} custom-call(bf16[8,1024,2048]{2,1,0:T(8,128)(2,1)} %volts_ref.3, f32[64,2048]{1,0:T(8,128)} %constant.18.clone.wave_ref, f32[4,2048]{1,0:T(4,128)} %fir_ref.3, f32[3,64,1024]{2,1,0:T(8,128)} %get-tuple-element.6.own_ref), custom_call_target="tpu_custom_call" | custom-call | flops 5368709120 | bytes 20971520 | tf_op jit(solution)/shard_map/pallas_call | solution.py:178
  30.8 0.0 collective-permute-done.carried_ref
  30.8 0.0 copy-start.1
  30.8 0.7 copy-done.1
  31.6 3.5 %shard_map.79 = bf16[512,1024]{1,0:T(8,128)(2,1)} custom-call(f32[8,64,1024]{2,1,0:T(8,128)} %shard_map.78.sum_ref, bf16[3,64,1024]{2,1,0:T(8,128)(2,1)} %copy-done.1), custom_call_target="tpu_custom_call" | custom-call | tf_op jit(solution)/shard_map/pallas_call | solution.py:212
  35.0 7.1 %all-to-all-start = ((bf16[32,16,1024]{2,1,0:T(8,128)(2,1)}), bf16[32,16,1024]{2,1,0:T(8,128)(2,1)S(1)}, u32[]{:S(2)}, u32[]{:S(2)}) async-start(bf16[32,16,1024]{2,1,0:T(8,128)(2,1)} %bitcast.6), calls=%async_computation | async-start | bytes 2097152 | tf_op jit(solution)/shard_map/all_to_all | solution.py:220
  42.1 0.0 copy-done.2
  42.2 1.0 %multiply_convert_fusion.1 = (bf16[32,2048]{1,0:T(8,128)(2,1)S(1)}, bf16[32,2048]{1,0:T(8,128)(2,1)S(1)}) fusion(f32[32,2048]{1,0:T(8,128)S(1)} %copy-done.2, f32[]{:T(128)S(6)} %convert_element_type.4), kind=kLoop, calls=%fused_computation.2 | loop fusion | flops 393216 | bytes 524292 | tf_op jit(solution)/shard_map/convert
  43.2 0.7 pad_maximum_fusion.weight_ref
  43.9 24.5 %all-to-all-done = bf16[32,16,1024]{2,1,0:T(8,128)(2,1)S(1)} async-done(((bf16[32,16,1024]{2,1,0:T(8,128)(2,1)}), bf16[32,16,1024]{2,1,0:T(8,128)(2,1)S(1)}, u32[]{:S(2)}, u32[]{:S(2)}) %all-to-all-start) | async-done | bytes 1048608 | tf_op jit(solution)/shard_map/all_to_all | solution.py:220
  68.4 0.0 copy-start
  68.4 1.0 %copy-done = bf16[32,16,1024]{2,1,0:T(8,128)(2,1)} copy-done((bf16[32,16,1024]{2,1,0:T(8,128)(2,1)}, bf16[32,16,1024]{2,1,0:T(8,128)(2,1)S(1)}, u32[]{:S(2)}) %copy-start) | copy-done | bytes 1048600
  69.3 11.1 %shard_map.80 = (bf16[2048,2048]{1,0:T(8,128)(2,1)}, bf16[2,1024,128]{2,1,0:T(8,128)(2,1)}) custom-call(bf16[16,2,16,1024]{3,2,1,0:T(8,128)(2,1)} %bitcast.7, s32[1,2048]{1,0:T(1,128)} %bitcast.8, bf16[64,2048]{1,0:T(8,128)(2,1)} %pad_maximum_fusion.weight_ref, s32[1,1024]{1,0:T(1,128)} %bitcast.9), custom_call_target="tpu_custom_call" | custom-call | tf_op jit(solution)/shard_map/pallas_call | solution.py:237
Async XLA Ops:
  11.4 19.4 %collective-permute-start = (bf16[3,64,1024]{2,1,0:T(8,128)(2,1)}, bf16[3,64,1024]{2,1,0:T(8,128)(2,1)S(1)}, u32[]{:S(2)}, u32[]{:S(2)}) collective-permute-start(bf16[3,64,1024]{2,1,0:T(8,128)(2,1)} %get-tuple-element.7), channel_id=1, source_target_pairs={{0,2},{2,4},{4,6},{6,8},{8,10},{10,12},{12,14},{14,16},{16,18},{18... | collective-permute-start | bytes 1179656 | tf_op jit(solution)/shard_map/ppermute | solution.py:205
  13.8 28.3 %copy-start.2 = (f32[32,2048]{1,0:T(8,128)S(1)}, f32[32,2048]{1,0:T(8,128)}, u32[]{:S(2)}) copy-start(f32[32,2048]{1,0:T(8,128)} %param.8) | copy-start | bytes 786436
  30.8 0.7 copy-start.1
  35.0 33.4 %all-to-all-start = ((bf16[32,16,1024]{2,1,0:T(8,128)(2,1)}), bf16[32,16,1024]{2,1,0:T(8,128)(2,1)S(1)}, u32[]{:S(2)}, u32[]{:S(2)}) async-start(bf16[32,16,1024]{2,1,0:T(8,128)(2,1)} %bitcast.6), calls=%async_computation | async-start | bytes 2097152 | tf_op jit(solution)/shard_map/all_to_all | solution.py:220
  68.4 1.0 %copy-start = (bf16[32,16,1024]{2,1,0:T(8,128)(2,1)}, bf16[32,16,1024]{2,1,0:T(8,128)(2,1)S(1)}, u32[]{:S(2)}) copy-start(bf16[32,16,1024]{2,1,0:T(8,128)(2,1)S(1)} %all-to-all-done) | copy-start | bytes 3145732

commit v2 on v1

v2 whole, which is shorter than its diff:
```python
import functools
import math

import jax
import jax.numpy as jnp
import numpy as np
from jax import lax
from jax.experimental import pallas as pl
from jax.experimental.pallas import tpu as pltpu
from jax.sharding import PartitionSpec as P

MINOR = (((1,), (1,)), ((), ()))
MAJOR = (((0,), (0,)), ((), ()))
LANES = 128
AHEAD = 8


def fourier_table(frame, first, channels):
    turns = np.arange(first, first + channels)[:, None] * np.arange(frame)[None, :] % frame
    angle = turns * (2.0 * math.pi / frame)
    factor = 1.0 / math.sqrt(frame)
    pair = np.stack([np.cos(angle) * factor, -np.sin(angle) * factor], axis=1)
    return pair.reshape(2 * channels, frame).astype(np.float32)


def frame_products(frames, taps, volts_ref, table, held, sems, block, prepare, emit):
    rows = table.shape[0] // taps
    inputs = volts_ref.shape[1]
    count = len(frames)
    unit = block // 2 if block % (2 * LANES) == 0 else block
    per = block // unit
    copies = []
    for start in range(0, inputs, block):
        for k in range(count):
            for at in range(start, start + block, unit):
                place = len(copies)
                copies.append(
                    pltpu.make_async_copy(
                        volts_ref.at[frames[k], pl.ds(at, unit)],
                        held.at[k, pl.ds(at, unit)],
                        sems.at[place],
                    )
                )
    for copy in copies[:AHEAD]:
        copy.start()
    prepare()
    done = 0
    for start in range(0, inputs, block):
        sums = {}
        for k in range(count):
            for copy in copies[done : done + per]:
                copy.wait()
            for copy in copies[done + AHEAD : done + AHEAD + per]:
                copy.start()
            done += per
            terms = lax.dot_general(
                table[...],
                held[k, start : start + block],
                MINOR,
                preferred_element_type=jnp.float32,
            )
            for m in range(taps):
                part = terms[m * rows : (m + 1) * rows]
                at = frames[k] + m
                sums[at] = sums[at] + part if at in sums else part
        emit(slice(start, start + block), sums)


def last_frames_kernel(
    total, taps, block, volts_ref, wave_hbm, fir_hbm, own_ref, tail_ref, table, held, sems,
    wave, fir, extra,
):
    lag = taps - 1
    rows = wave.shape[0]
    loads = [
        pltpu.make_async_copy(wave_hbm, wave, extra.at[0]),
        pltpu.make_async_copy(fir_hbm, fir, extra.at[1]),
    ]
    for load in loads:
        load.start()

    def prepare():
        for load in loads:
            load.wait()
        for m in range(taps):
            table[m * rows : (m + 1) * rows, :] = (wave[...] * fir[m : m + 1, :]).astype(table.dtype)

    def emit(at, sums):
        for k in range(lag):
            own_ref[k, :, at] = sums[total - lag + k]
            tail_ref[k, :, at] = sums[total + k].astype(tail_ref.dtype)

    frames = list(range(total - lag, total))
    frame_products(frames, taps, volts_ref, table, held, sems, block, prepare, emit)


def first_frames_kernel(total, taps, block, volts_ref, table_ref, own_ref, sum_ref, held, sems):
    lag = taps - 1

    def emit(at, sums):
        for t in range(total):
            value = sums[t]
            if t >= total - lag:
                value = value + own_ref[t - (total - lag), :, at]
            sum_ref[t, :, at] = value

    frames = list(range(total - lag))
    frame_products(frames, taps, volts_ref, table_ref, held, sems, block, lambda: None, emit)


def join_kernel(sum_ref, carried_ref, out_ref, rows):
    total, count = sum_ref.shape[0], sum_ref.shape[1]
    lag = carried_ref.shape[0]
    for t in range(total):
        value = sum_ref[t]
        if t < lag:
            value = value + carried_ref[t].astype(jnp.float32)
        for j in range(rows.shape[0]):
            rows[j, pl.ds(t, count, stride=total), :] = value[:, j * LANES : (j + 1) * LANES]
    for j in range(rows.shape[0]):
        out_ref[:, j * LANES : (j + 1) * LANES] = rows[j].astype(out_ref.dtype)


def channel_kernel(
    scale, block, got_ref, order_ref, weight_ref, dir_ref, vis_hbm, beam_ref,
    flat, mixed, turned, across, vis, sems,
):
    sections, chans, pair, inputs = got_ref.shape
    frames = sections * pair // 2
    total = flat.shape[1]
    for c in range(chans):
        flat[:, c * inputs : (c + 1) * inputs] = got_ref[:, c].reshape(2 * frames, inputs)
    for start in range(0, total, block):
        at = slice(start, start + block)
        source = lax.broadcasted_iota(jnp.int32, (total, block), 0)
        chosen = (source == order_ref[:, at]).astype(jnp.bfloat16)
        picked = jnp.dot(flat[...], chosen, preferred_element_type=jnp.float32)
        parts = picked.reshape(sections, 2, pair // 2, block)
        real = parts[:, 0].reshape(frames, block)
        imag = parts[:, 1].reshape(frames, block)
        both = jnp.concatenate([real, imag], axis=0).astype(mixed.dtype)
        mixed[:, at] = both
        turned[:, at] = jnp.concatenate([-imag, real], axis=0).astype(turned.dtype)
        across[at, :] = both.T
    copies = []
    for start in range(0, total, block):
        at = slice(start, start + block)
        end = start + block
        above = jnp.dot(across[:end], mixed[:, at], preferred_element_type=jnp.float32)
        below = jnp.dot(across[start:], turned[:, at], preferred_element_type=jnp.float32)
        row = lax.broadcasted_iota(jnp.int32, (block, block), 0)
        col = lax.broadcasted_iota(jnp.int32, (block, block), 1)
        crossing = jnp.where(col >= row, above[start:], below[:block])
        if start > 0:
            vis[:start, at] = (above[:start] * scale).astype(vis.dtype)
        vis[at, at] = (crossing * scale).astype(vis.dtype)
        if end < total:
            vis[end:, at] = (below[block:] * scale).astype(vis.dtype)
        copies.append(pltpu.make_async_copy(vis.at[:, at], vis_hbm.at[:, at], sems.at[len(copies)]))
        copies[-1].start()
    mix = jnp.dot(weight_ref[...], across[...], preferred_element_type=jnp.float32)
    dirs = mix.shape[0] // 2
    beam_real = mix[:dirs, :frames] - mix[dirs:, frames:]
    beam_imag = mix[:dirs, frames:] + mix[dirs:, :frames]
    formed = jnp.concatenate([beam_real, beam_imag], axis=1).astype(jnp.bfloat16)
    beams = beam_ref.shape[1]
    row = lax.broadcasted_iota(jnp.int32, (dirs, beams), 0)
    chosen = (row == dir_ref[...]).astype(jnp.bfloat16)
    spread = lax.dot_general(chosen, formed, MAJOR, preferred_element_type=jnp.float32)
    beam_ref[0] = spread[:, :frames].astype(beam_ref.dtype)
    beam_ref[1] = spread[:, frames:].astype(beam_ref.dtype)
    for copy in copies:
        copy.wait()


def on_device(voltages, fir_taps, steer, beam_dir, input_order):
    section_count = lax.axis_size("section")
    chan_count = lax.axis_size("chan")
    devices = section_count * chan_count
    spec_dev, inputs_here, frame = voltages.shape
    taps = fir_taps.shape[0]
    lag = taps - 1
    channels = devices
    first = frame // 8
    rows = 2 * channels
    total_inputs = inputs_here * chan_count
    total_frames = spec_dev * section_count
    wave = jnp.asarray(fourier_table(frame, first, channels))
    block = min(512, inputs_here)
    whole = pl.BlockSpec(memory_space=pltpu.VMEM)

    stay = pl.BlockSpec(memory_space=pltpu.HBM)

    def call(kernel, frames, operands, specs, outs, scratch):
        held = frames * inputs_here * frame * voltages.dtype.itemsize
        limit = held + 2 * taps * rows * frame * 2 + (12 << 20)
        return pl.pallas_call(
            functools.partial(kernel, spec_dev, taps, block),
            in_specs=specs,
            out_specs=[whole] * len(outs),
            out_shape=outs,
            scratch_shapes=[
                pltpu.VMEM((frames, inputs_here, frame), voltages.dtype),
                pltpu.SemaphoreType.DMA((2 * frames * inputs_here // block,)),
                *scratch,
            ],
            compiler_params=pltpu.CompilerParams(vmem_limit_bytes=limit),
            cost_estimate=pl.CostEstimate(
                flops=2 * taps * rows * frame * inputs_here * frames,
                bytes_accessed=held,
                transcendentals=0,
            ),
        )(*operands)

    keep = lambda x: pltpu.with_memory_space_constraint(x, pltpu.HBM)
    own, tail, table = call(
        last_frames_kernel,
        lag,
        (voltages, keep(wave), keep(fir_taps)),
        [stay, stay, stay],
        [
            jax.ShapeDtypeStruct((lag, rows, inputs_here), jnp.float32),
            jax.ShapeDtypeStruct((lag, rows, inputs_here), jnp.bfloat16),
            jax.ShapeDtypeStruct((taps * rows, frame), jnp.bfloat16),
        ],
        [
            pltpu.VMEM(wave.shape, wave.dtype),
            pltpu.VMEM(fir_taps.shape, fir_taps.dtype),
            pltpu.SemaphoreType.DMA((2,)),
        ],
    )
    carried = lax.ppermute(tail, "section", [(i, i + 1) for i in range(section_count - 1)])
    (sums,) = call(
        first_frames_kernel,
        spec_dev - lag,
        (voltages, table, own),
        [stay, whole, whole],
        [jax.ShapeDtypeStruct((spec_dev, rows, inputs_here), jnp.float32)],
        [],
    )
    spectra = pl.pallas_call(
        join_kernel,
        in_specs=[whole] * 2,
        out_specs=whole,
        out_shape=jax.ShapeDtypeStruct((rows * spec_dev, inputs_here), jnp.bfloat16),
        scratch_shapes=[pltpu.VMEM((inputs_here // LANES, rows * spec_dev, LANES), jnp.float32)],
        compiler_params=pltpu.CompilerParams(vmem_limit_bytes=12 << 20),
    )(sums, carried)
    got = lax.all_to_all(
        spectra.reshape(devices, 2 * spec_dev, inputs_here),
        ("section", "chan"),
        split_axis=0,
        concat_axis=0,
        tiled=True,
    ).reshape(section_count, chan_count, 2 * spec_dev, inputs_here)

    channel = lax.axis_index("section") * chan_count + lax.axis_index("chan")
    phase = steer * (first + channel).astype(jnp.float32)
    size = math.sqrt(total_inputs)
    weights = jnp.concatenate([jnp.cos(phase) / size, -jnp.sin(phase) / size], axis=0).astype(
        jnp.bfloat16
    )
    beam_count = beam_dir.shape[0]
    block = min(256, total_inputs)
    lanes = 2 * total_frames
    vis, beams = pl.pallas_call(
        functools.partial(channel_kernel, 1.0 / math.sqrt(total_frames), block),
        in_specs=[whole] * 4,
        out_specs=[pl.BlockSpec(memory_space=pl.ANY), whole],
        out_shape=[
            jax.ShapeDtypeStruct((total_inputs, total_inputs), jnp.bfloat16),
            jax.ShapeDtypeStruct((2, beam_count, total_frames), jnp.bfloat16),
        ],
        scratch_shapes=[
            pltpu.VMEM((lanes, total_inputs), jnp.bfloat16),
            pltpu.VMEM((lanes, total_inputs), jnp.bfloat16),
            pltpu.VMEM((lanes, total_inputs), jnp.bfloat16),
            pltpu.VMEM((total_inputs, lanes), jnp.bfloat16),
            pltpu.VMEM((total_inputs, total_inputs), jnp.bfloat16),
            pltpu.SemaphoreType.DMA((total_inputs // block,)),
        ],
        compiler_params=pltpu.CompilerParams(vmem_limit_bytes=32 << 20),
    )(got, input_order.reshape(1, total_inputs), weights, beam_dir.reshape(1, beam_count))
    return (vis[None], beams[None])


def solution(mesh):
    return jax.shard_map(
        on_device,
        mesh=mesh,
        in_specs=(P("section", "chan", None), P(), P(), P(), P()),
        out_specs=(P(("section", "chan"), None, None), P(("section", "chan"), None, None, None)),
        check_vma=False,
    )
```

time: 80.8 us -> 62.4 us (0.77)
  Pallas kernels: 42.4 us -> 25.6 us
  local copies, waits for them, and re-layouts: 1.71 us -> 0.02 us
    pallas_call x2, Pallas kernels: 27.8 us -> 16.5 us  [call(): pl.pallas_call(functools.partial(kernel, spec_dev, taps, block), in_specs...]
    pallas_call x1, Pallas kernels: 11.1 us -> 7.3 us  [on_device(): pl.pallas_call(functools.partial(channel_kernel, 1.0 / math.sqrt(total_fr...]
    unnamed x6, local copies, waits for them, and re-layouts: 1.71 us -> 0.02 us
    pallas_call x1, Pallas kernels: 3.45 us -> 1.83 us  [on_device(): pl.pallas_call(join_kernel, in_specs=[whole] * 2, out_specs=whole, out_sh...]
  transfers between devices with their start and end apart: 2 -> 2, of which waited for: 1 -> 1; matrix products, arithmetic and copies ran while one was open for 2% -> 2% of each run, Pallas kernels for 21% -> 14%
where the time goes in v2:
time: 62.4 us; the launch traced here: 62.2 us
  Pallas kernels  25.6 us (41%)
  waiting for transfers between devices  25 us (40%)
  starting transfers between devices  9.67 us (15%)
  other arithmetic  1.01 us (2%)
  between operations  0.89 us (1%)
    all_to_all x1, waiting for transfers between devices, on_device(): lax.all_to_all(spectra.reshape(devices, 2 * spec_dev, inputs_here), ('sec...  25 us
    pallas_call x2, Pallas kernels, call(): pl.pallas_call(functools.partial(kernel, spec_dev, taps, block), in_specs...  16.5 us
    pallas_call x1, Pallas kernels, on_device(): pl.pallas_call(functools.partial(channel_kernel, 1.0 / math.sqrt(total_fr...  7.3 us
    all_to_all x1, starting transfers between devices, on_device(): lax.all_to_all(spectra.reshape(devices, 2 * spec_dev, inputs_here), ('sec...  7.29 us
    ppermute x1, starting transfers between devices, on_device(): lax.ppermute(tail, 'section', [(i, i + 1) for i in range(section_count -...  2.38 us
    pallas_call x1, Pallas kernels, on_device(): pl.pallas_call(join_kernel, in_specs=[whole] * 2, out_specs=whole, out_sh...  1.83 us
  transfers between devices with their start and end apart: 2, of which 1 were waited for; matrix products, arithmetic and copies ran while one was open for 2% of the time, Pallas kernels for 14%

profile of v2, /device:TPU:0, one launch (start us, length us, event | category | flops | bytes accessed | tf_op | source)
XLA Modules:
  0.0 62.2 jit_solution(13970604983274581752)
XLA Ops:
  0.6 7.6 %shard_map.77 = (f32[3,64,1024]{2,1,0:T(8,128)S(1)}, bf16[3,64,1024]{2,1,0:T(8,128)(2,1)S(1)}, bf16[256,2048]{1,0:T(8,128)(2,1)S(1)}) custom-call(bf16[8,1024,2048]{2,1,0:T(8,128)(2,1)} %volts_ref.3, f32[64,2048]{1,0:T(8,128)} %constant.18.clone.wave_hbm, f32[4,2048]{1,0:T(4,128)} %fir_hbm.1), custom_call_target="tpu_custom_call" | custom-call | flops 3221225472 | bytes 12582912 | tf_op jit(solution)/shard_map/pallas_call | solution.py:197
  8.2 2.4 %collective-permute-start = (bf16[3,64,1024]{2,1,0:T(8,128)(2,1)S(1)}, bf16[3,64,1024]{2,1,0:T(8,128)(2,1)S(1)}, u32[]{:S(2)}, u32[]{:S(2)}) collective-permute-start(bf16[3,64,1024]{2,1,0:T(8,128)(2,1)S(1)} %get-tuple-element.9), channel_id=1, source_target_pairs={{0,2},{2,4},{4,6},{6,8},{8,10},{10,12},{12,14},{14,16},{16,18},{18... | collective-permute-start | bytes 1179656 | tf_op jit(solution)/shard_map/ppermute | solution.py:232
  10.6 0.0 copy-start.2
  10.6 0.0 copy-start
  10.7 0.0 copy-start.1
  10.7 8.9 %shard_map.78.sum_ref = f32[8,64,1024]{2,1,0:T(8,128)S(1)} custom-call(bf16[8,1024,2048]{2,1,0:T(8,128)(2,1)} %volts_ref.3, bf16[256,2048]{1,0:T(8,128)(2,1)S(1)} %get-tuple-element.7.table_ref, f32[3,64,1024]{2,1,0:T(8,128)S(1)} %get-tuple-element.8.own_ref), custom_call_target="tpu_custom_call" | custom-call | flops 5368709120 | bytes 20971520 | tf_op jit(solution)/shard_map/pallas_call | solution.py:197
  19.5 0.0 collective-permute-done.carried_ref
  19.5 1.8 %shard_map.79 = bf16[512,1024]{1,0:T(8,128)(2,1)} custom-call(f32[8,64,1024]{2,1,0:T(8,128)S(1)} %shard_map.78.sum_ref, bf16[3,64,1024]{2,1,0:T(8,128)(2,1)S(1)} %collective-permute-done.carried_ref), custom_call_target="tpu_custom_call" | custom-call | tf_op jit(solution)/shard_map/pallas_call | solution.py:241
  21.4 7.3 %all-to-all-start = ((bf16[32,16,1024]{2,1,0:T(8,128)(2,1)}), bf16[32,16,1024]{2,1,0:T(8,128)(2,1)S(1)}, u32[]{:S(2)}, u32[]{:S(2)}) async-start(bf16[32,16,1024]{2,1,0:T(8,128)(2,1)} %bitcast), calls=%async_computation | async-start | bytes 2097152 | tf_op jit(solution)/shard_map/all_to_all | solution.py:249
  28.7 0.0 copy-done.2
  28.7 1.0 %multiply_convert_fusion.1 = (bf16[32,2048]{1,0:T(8,128)(2,1)S(1)}, bf16[32,2048]{1,0:T(8,128)(2,1)S(1)}) fusion(f32[32,2048]{1,0:T(8,128)S(1)} %copy-done.2, f32[]{:T(128)S(6)} %convert_element_type.4), kind=kLoop, calls=%fused_computation.2 | loop fusion | flops 393216 | bytes 524292 | tf_op jit(solution)/shard_map/convert
  29.7 25.0 %all-to-all-done = bf16[32,16,1024]{2,1,0:T(8,128)(2,1)S(1)} async-done(((bf16[32,16,1024]{2,1,0:T(8,128)(2,1)}), bf16[32,16,1024]{2,1,0:T(8,128)(2,1)S(1)}, u32[]{:S(2)}, u32[]{:S(2)}) %all-to-all-start) | async-done | bytes 1048608 | tf_op jit(solution)/shard_map/all_to_all | solution.py:249
  54.7 0.0 copy-done
  54.7 0.0 copy-done.1
  54.7 7.3 %shard_map.80 = (bf16[2048,2048]{1,0:T(8,128)(2,1)}, bf16[2,1024,128]{2,1,0:T(8,128)(2,1)}) custom-call(bf16[16,2,16,1024]{3,2,1,0:T(8,128)(2,1)S(1)} %bitcast.6, s32[1,2048]{1,0:T(1,128)S(1)} %bitcast.7, bf16[64,2048]{1,0:T(8,128)(2,1)S(1)} %pad_maximum_fusion.weight_ref, s32[1,1024]{1,0:T(1,128)S(1)} %bitcast.8), custom_call_target="tpu_custom_call" | custom-call | tf_op jit(solution)/shard_map/pallas_call | solution.py:266
  (1 shorter events, 0.0 us)
Async XLA Ops:
  8.2 11.3 %collective-permute-start = (bf16[3,64,1024]{2,1,0:T(8,128)(2,1)S(1)}, bf16[3,64,1024]{2,1,0:T(8,128)(2,1)S(1)}, u32[]{:S(2)}, u32[]{:S(2)}) collective-permute-start(bf16[3,64,1024]{2,1,0:T(8,128)(2,1)S(1)} %get-tuple-element.9), channel_id=1, source_target_pairs={{0,2},{2,4},{4,6},{6,8},{8,10},{10,12},{12,14},{14,16},{16,18},{18... | collective-permute-start | bytes 1179656 | tf_op jit(solution)/shard_map/ppermute | solution.py:232
  10.6 18.0 %copy-start.2 = (f32[32,2048]{1,0:T(8,128)S(1)}, f32[32,2048]{1,0:T(8,128)}, u32[]{:S(2)}) copy-start(f32[32,2048]{1,0:T(8,128)} %param.8) | copy-start | bytes 786436
  10.6 44.1 %copy-start = (s32[2048]{0:T(1024)S(1)}, s32[2048]{0:T(1024)}, u32[]{:S(2)}) copy-start(s32[2048]{0:T(1024)} %param.10) | copy-start | bytes 24580
  10.7 44.1 %copy-start.1 = (s32[1024]{0:T(1024)S(1)}, s32[1024]{0:T(1024)}, u32[]{:S(2)}) copy-start(s32[1024]{0:T(1024)} %param.9) | copy-start | bytes 12292
  21.4 33.4 %all-to-all-start = ((bf16[32,16,1024]{2,1,0:T(8,128)(2,1)}), bf16[32,16,1024]{2,1,0:T(8,128)(2,1)S(1)}, u32[]{:S(2)}, u32[]{:S(2)}) async-start(bf16[32,16,1024]{2,1,0:T(8,128)(2,1)} %bitcast), calls=%async_computation | async-start | bytes 2097152 | tf_op jit(solution)/shard_map/all_to_all | solution.py:249

commit v3 on v2

--- a/solution.py
+++ b/solution.py
@@ -3,7 +3,6 @@
 
 import jax
 import jax.numpy as jnp
-import numpy as np
 from jax import lax
 from jax.experimental import pallas as pl
 from jax.experimental.pallas import tpu as pltpu
@@ -12,23 +11,43 @@
 MINOR = (((1,), (1,)), ((), ()))
 MAJOR = (((0,), (0,)), ((), ()))
 LANES = 128
-AHEAD = 8
-
-
-def fourier_table(frame, first, channels):
-    turns = np.arange(first, first + channels)[:, None] * np.arange(frame)[None, :] % frame
-    angle = turns * (2.0 * math.pi / frame)
+AHEAD = 4
+EARLY = 2
+
+
+def fourier_rows(frame, first, channels):
+    shape = (channels, frame)
+    samples = lax.broadcasted_iota(jnp.int32, shape, 1)
+    bins = lax.broadcasted_iota(jnp.int32, shape, 0) + first
+    quarter = frame // 4
+    if frame & (frame - 1):
+        turns = lax.rem(bins * samples, frame)
+        quadrant = lax.div(turns + quarter // 2, quarter)
+    else:
+        turns = (bins * samples) & (frame - 1)
+        quadrant = (turns + quarter // 2) >> (quarter.bit_length() - 1)
+    angle = (turns - quadrant * quarter).astype(jnp.float32) * (2.0 * math.pi / frame)
+    square = angle * angle
+    sine = 1.0 / 362880.0
+    for term in (-1.0 / 5040.0, 1.0 / 120.0, -1.0 / 6.0, 1.0):
+        sine = sine * square + term
+    sine = sine * angle
+    cosine = 1.0 / 40320.0
+    for term in (-1.0 / 720.0, 1.0 / 24.0, -0.5, 1.0):
+        cosine = cosine * square + term
     factor = 1.0 / math.sqrt(frame)
-    pair = np.stack([np.cos(angle) * factor, -np.sin(angle) * factor], axis=1)
-    return pair.reshape(2 * channels, frame).astype(np.float32)
+    odd = (quadrant & 1) == 1
+    real = jnp.where(odd, sine, cosine) * jnp.where(((quadrant + 1) & 2) == 2, -factor, factor)
+    imag = jnp.where(odd, cosine, sine) * jnp.where((quadrant & 2) == 2, factor, -factor)
+    return real, imag
 
 
 def frame_products(frames, taps, volts_ref, table, held, sems, block, prepare, emit):
     rows = table.shape[0] // taps
     inputs = volts_ref.shape[1]
     count = len(frames)
-    unit = block // 2 if block % (2 * LANES) == 0 else block
-    per = block // unit
+    unit = block
+    per = 1
     copies = []
     for start in range(0, inputs, block):
         for k in range(count):
@@ -41,9 +60,11 @@
                         sems.at[place],
                     )
                 )
-    for copy in copies[:AHEAD]:
+    for copy in copies[:EARLY]:
         copy.start()
     prepare()
+    for copy in copies[EARLY:AHEAD]:
+        copy.start()
     done = 0
     for start in range(0, inputs, block):
         sums = {}
@@ -67,23 +88,26 @@
 
 
 def last_frames_kernel(
-    total, taps, block, volts_ref, wave_hbm, fir_hbm, own_ref, tail_ref, table, held, sems,
-    wave, fir, extra,
+    first, total, taps, block, volts_ref, fir_hbm, own_ref, tail_ref, table, held, sems,
+    fir, loaded,
 ):
     lag = taps - 1
-    rows = wave.shape[0]
-    loads = [
-        pltpu.make_async_copy(wave_hbm, wave, extra.at[0]),
-        pltpu.make_async_copy(fir_hbm, fir, extra.at[1]),
-    ]
-    for load in loads:
-        load.start()
+    rows, frame = table.shape[0] // taps, table.shape[1]
+    load = pltpu.make_async_copy(fir_hbm, fir, loaded)
+    load.start()
 
     def prepare():
-        for load in loads:
-            load.wait()
-        for m in range(taps):
-            table[m * rows : (m + 1) * rows, :] = (wave[...] * fir[m : m + 1, :]).astype(table.dtype)
+        step = min(rows // 2, 8)
+        for start in range(0, rows // 2, step):
+            real, imag = fourier_rows(frame, first + start, step)
+            if start == 0:
+                load.wait()
+            for m in range(taps):
+                row = fir[m : m + 1, :]
+                at = m * rows + start
+                table[at : at + step, :] = (real * row).astype(table.dtype)
+                at += rows // 2
+                table[at : at + step, :] = (imag * row).astype(table.dtype)
 
     def emit(at, sums):
         for k in range(lag):
@@ -108,17 +132,27 @@
     frame_products(frames, taps, volts_ref, table_ref, held, sems, block, lambda: None, emit)
 
 
-def join_kernel(sum_ref, carried_ref, out_ref, rows):
-    total, count = sum_ref.shape[0], sum_ref.shape[1]
+def join_kernel(sum_ref, carried_ref, out_hbm, rows, out, sems):
+    total, count = sum_ref.shape[0], sum_ref.shape[1] // 2
     lag = carried_ref.shape[0]
-    for t in range(total):
-        value = sum_ref[t]
-        if t < lag:
-            value = value + carried_ref[t].astype(jnp.float32)
-        for j in range(rows.shape[0]):
-            rows[j, pl.ds(t, count, stride=total), :] = value[:, j * LANES : (j + 1) * LANES]
+    per = rows.shape[0] // sems.shape[0]
+    copies = []
     for j in range(rows.shape[0]):
-        out_ref[:, j * LANES : (j + 1) * LANES] = rows[j].astype(out_ref.dtype)
+        at = slice(j * LANES, (j + 1) * LANES)
+        for t in range(total):
+            value = sum_ref[t, :, at]
+            if t < lag:
+                value = value + carried_ref[t, :, at].astype(jnp.float32)
+            for part in range(2):
+                spot = pl.ds(part * total + t, count, stride=2 * total)
+                rows[j, spot, :] = value[part * count : (part + 1) * count]
+        out[:, at] = rows[j].astype(out.dtype)
+        if (j + 1) % per == 0:
+            at = slice((j + 1 - per) * LANES, (j + 1) * LANES)
+            copies.append(pltpu.make_async_copy(out.at[:, at], out_hbm.at[:, at], sems.at[j // per]))
+            copies[-1].start()
+    for copy in copies:
+        copy.wait()
 
 
 def channel_kernel(
@@ -185,7 +219,6 @@
     rows = 2 * channels
     total_inputs = inputs_here * chan_count
     total_frames = spec_dev * section_count
-    wave = jnp.asarray(fourier_table(frame, first, channels))
     block = min(512, inputs_here)
     whole = pl.BlockSpec(memory_space=pltpu.VMEM)
 
@@ -201,7 +234,7 @@
             out_shape=outs,
             scratch_shapes=[
                 pltpu.VMEM((frames, inputs_here, frame), voltages.dtype),
-                pltpu.SemaphoreType.DMA((2 * frames * inputs_here // block,)),
+                pltpu.SemaphoreType.DMA((frames * inputs_here // block,)),
                 *scratch,
             ],
             compiler_params=pltpu.CompilerParams(vmem_limit_bytes=limit),
@@ -214,19 +247,18 @@
 
     keep = lambda x: pltpu.with_memory_space_constraint(x, pltpu.HBM)
     own, tail, table = call(
-        last_frames_kernel,
+        functools.partial(last_frames_kernel, first),
         lag,
-        (voltages, keep(wave), keep(fir_taps)),
-        [stay, stay, stay],
+        (voltages, keep(fir_taps)),
+        [stay, stay],
         [
             jax.ShapeDtypeStruct((lag, rows, inputs_here), jnp.float32),
             jax.ShapeDtypeStruct((lag, rows, inputs_here), jnp.bfloat16),
             jax.ShapeDtypeStruct((taps * rows, frame), jnp.bfloat16),
         ],
         [
-            pltpu.VMEM(wave.shape, wave.dtype),
             pltpu.VMEM(fir_taps.shape, fir_taps.dtype),
-            pltpu.SemaphoreType.DMA((2,)),
+            pltpu.SemaphoreType.DMA,
         ],
     )
     carried = lax.ppermute(tail, "section", [(i, i + 1) for i in range(section_count - 1)])
@@ -238,12 +270,17 @@
         [jax.ShapeDtypeStruct((spec_dev, rows, inputs_here), jnp.float32)],
         [],
     )
+    lane_blocks = inputs_here // LANES
     spectra = pl.pallas_call(
         join_kernel,
         in_specs=[whole] * 2,
-        out_specs=whole,
+        out_specs=pl.BlockSpec(memory_space=pl.ANY),
         out_shape=jax.ShapeDtypeStruct((rows * spec_dev, inputs_here), jnp.bfloat16),
-        scratch_shapes=[pltpu.VMEM((inputs_here // LANES, rows * spec_dev, LANES), jnp.float32)],
+        scratch_shapes=[
+            pltpu.VMEM((lane_blocks, rows * spec_dev, LANES), jnp.float32),
+            pltpu.VMEM((rows * spec_dev, inputs_here), jnp.bfloat16),
+            pltpu.SemaphoreType.DMA((min(4, lane_blocks),)),
+        ],
         compiler_params=pltpu.CompilerParams(vmem_limit_bytes=12 << 20),
     )(sums, carried)
     got = lax.all_to_all(

time: 62.4 us -> 61 us (0.978)
  Pallas kernels: 25.6 us -> 24.1 us
    pallas_call x2, Pallas kernels: 16.5 us -> 14.9 us  [call(): pl.pallas_call(functools.partial(kernel, spec_dev, taps, block), in_specs...]
where the time goes in v3:
time: 61 us; the launch traced here: 60.8 us
  waiting for transfers between devices  25 us (41%)
  Pallas kernels  24.1 us (40%)
  starting transfers between devices  9.68 us (16%)
  other arithmetic  1.01 us (2%)
  between operations  0.89 us (1%)
    all_to_all x1, waiting for transfers between devices, on_device(): lax.all_to_all(spectra.reshape(devices, 2 * spec_dev, inputs_here), ('sec...  25 us
    pallas_call x2, Pallas kernels, call(): pl.pallas_call(functools.partial(kernel, spec_dev, taps, block), in_specs...  14.9 us
    pallas_call x1, Pallas kernels, on_device(): pl.pallas_call(functools.partial(channel_kernel, 1.0 / math.sqrt(total_fr...  7.3 us
    all_to_all x1, starting transfers between devices, on_device(): lax.all_to_all(spectra.reshape(devices, 2 * spec_dev, inputs_here), ('sec...  7.29 us
    ppermute x1, starting transfers between devices, on_device(): lax.ppermute(tail, 'section', [(i, i + 1) for i in range(section_count -...  2.39 us
    pallas_call x1, Pallas kernels, on_device(): pl.pallas_call(join_kernel, in_specs=[whole] * 2, out_specs=pl.BlockSpec(...  1.94 us
  transfers between devices with their start and end apart: 2, of which 1 were waited for; matrix products, arithmetic and copies ran while one was open for 2% of the time, Pallas kernels for 14%

profile of v3, /device:TPU:0, one launch (start us, length us, event | category | flops | bytes accessed | tf_op | source)
XLA Modules:
  0.0 60.8 jit_solution(5516749012348048257)
XLA Ops:
  0.6 6.1 %shard_map.68 = (f32[3,64,1024]{2,1,0:T(8,128)S(1)}, bf16[3,64,1024]{2,1,0:T(8,128)(2,1)S(1)}, bf16[256,2048]{1,0:T(8,128)(2,1)S(1)}) custom-call(bf16[8,1024,2048]{2,1,0:T(8,128)(2,1)} %volts_ref.3, f32[4,2048]{1,0:T(4,128)} %fir_hbm.1), custom_call_target="tpu_custom_call" | custom-call | flops 3221225472 | bytes 12582912 | tf_op jit(solution)/shard_map/pallas_call | solution.py:230
  6.8 2.4 %collective-permute-start = (bf16[3,64,1024]{2,1,0:T(8,128)(2,1)S(1)}, bf16[3,64,1024]{2,1,0:T(8,128)(2,1)S(1)}, u32[]{:S(2)}, u32[]{:S(2)}) collective-permute-start(bf16[3,64,1024]{2,1,0:T(8,128)(2,1)S(1)} %get-tuple-element.9), channel_id=1, source_target_pairs={{0,2},{2,4},{4,6},{6,8},{8,10},{10,12},{12,14},{14,16},{16,18},{18... | collective-permute-start | bytes 1179656 | tf_op jit(solution)/shard_map/ppermute | solution.py:264
  9.1 0.0 copy-start.2
  9.2 0.0 copy-start
  9.2 0.0 copy-start.1
  9.2 8.8 %shard_map.69.sum_ref = f32[8,64,1024]{2,1,0:T(8,128)S(1)} custom-call(bf16[8,1024,2048]{2,1,0:T(8,128)(2,1)} %volts_ref.3, bf16[256,2048]{1,0:T(8,128)(2,1)S(1)} %get-tuple-element.7.table_ref, f32[3,64,1024]{2,1,0:T(8,128)S(1)} %get-tuple-element.8.own_ref), custom_call_target="tpu_custom_call" | custom-call | flops 5368709120 | bytes 20971520 | tf_op jit(solution)/shard_map/pallas_call | solution.py:230
  18.0 0.0 collective-permute-done.carried_ref
  18.0 1.9 %shard_map.70 = bf16[512,1024]{1,0:T(8,128)(2,1)} custom-call(f32[8,64,1024]{2,1,0:T(8,128)S(1)} %shard_map.69.sum_ref, bf16[3,64,1024]{2,1,0:T(8,128)(2,1)S(1)} %collective-permute-done.carried_ref), custom_call_target="tpu_custom_call" | custom-call | tf_op jit(solution)/shard_map/pallas_call | solution.py:274
  19.9 7.3 %all-to-all-start = ((bf16[32,16,1024]{2,1,0:T(8,128)(2,1)}), bf16[32,16,1024]{2,1,0:T(8,128)(2,1)S(1)}, u32[]{:S(2)}, u32[]{:S(2)}) async-start(bf16[32,16,1024]{2,1,0:T(8,128)(2,1)} %bitcast), calls=%async_computation | async-start | bytes 2097152 | tf_op jit(solution)/shard_map/all_to_all | solution.py:286
  27.2 0.0 copy-done.2
  27.3 1.0 %multiply_convert_fusion.1 = (bf16[32,2048]{1,0:T(8,128)(2,1)S(1)}, bf16[32,2048]{1,0:T(8,128)(2,1)S(1)}) fusion(f32[32,2048]{1,0:T(8,128)S(1)} %copy-done.2, f32[]{:T(128)S(6)} %convert_element_type.4), kind=kLoop, calls=%fused_computation.2 | loop fusion | flops 393216 | bytes 524292 | tf_op jit(solution)/shard_map/convert
  28.3 25.0 %all-to-all-done = bf16[32,16,1024]{2,1,0:T(8,128)(2,1)S(1)} async-done(((bf16[32,16,1024]{2,1,0:T(8,128)(2,1)}), bf16[32,16,1024]{2,1,0:T(8,128)(2,1)S(1)}, u32[]{:S(2)}, u32[]{:S(2)}) %all-to-all-start) | async-done | bytes 1048608 | tf_op jit(solution)/shard_map/all_to_all | solution.py:286
  53.3 0.0 copy-done
  53.3 0.0 copy-done.1
  53.3 7.3 %shard_map.71 = (bf16[2048,2048]{1,0:T(8,128)(2,1)}, bf16[2,1024,128]{2,1,0:T(8,128)(2,1)}) custom-call(bf16[16,2,16,1024]{3,2,1,0:T(8,128)(2,1)S(1)} %bitcast.6, s32[1,2048]{1,0:T(1,128)S(1)} %bitcast.7, bf16[64,2048]{1,0:T(8,128)(2,1)S(1)} %pad_maximum_fusion.weight_ref, s32[1,1024]{1,0:T(1,128)S(1)} %bitcast.8), custom_call_target="tpu_custom_call" | custom-call | tf_op jit(solution)/shard_map/pallas_call | solution.py:303
  (1 shorter events, 0.0 us)
Async XLA Ops:
  6.8 11.2 %collective-permute-start = (bf16[3,64,1024]{2,1,0:T(8,128)(2,1)S(1)}, bf16[3,64,1024]{2,1,0:T(8,128)(2,1)S(1)}, u32[]{:S(2)}, u32[]{:S(2)}) collective-permute-start(bf16[3,64,1024]{2,1,0:T(8,128)(2,1)S(1)} %get-tuple-element.9), channel_id=1, source_target_pairs={{0,2},{2,4},{4,6},{6,8},{8,10},{10,12},{12,14},{14,16},{16,18},{18... | collective-permute-start | bytes 1179656 | tf_op jit(solution)/shard_map/ppermute | solution.py:264
  9.1 18.1 %copy-start.2 = (f32[32,2048]{1,0:T(8,128)S(1)}, f32[32,2048]{1,0:T(8,128)}, u32[]{:S(2)}) copy-start(f32[32,2048]{1,0:T(8,128)} %param.7) | copy-start | bytes 786436
  9.2 44.1 %copy-start = (s32[2048]{0:T(1024)S(1)}, s32[2048]{0:T(1024)}, u32[]{:S(2)}) copy-start(s32[2048]{0:T(1024)} %param.9) | copy-start | bytes 24580
  9.2 44.1 %copy-start.1 = (s32[1024]{0:T(1024)S(1)}, s32[1024]{0:T(1024)}, u32[]{:S(2)}) copy-start(s32[1024]{0:T(1024)} %param.8) | copy-start | bytes 12292
  19.9 33.4 %all-to-all-start = ((bf16[32,16,1024]{2,1,0:T(8,128)(2,1)}), bf16[32,16,1024]{2,1,0:T(8,128)(2,1)S(1)}, u32[]{:S(2)}, u32[]{:S(2)}) async-start(bf16[32,16,1024]{2,1,0:T(8,128)(2,1)} %bitcast), calls=%async_computation | async-start | bytes 2097152 | tf_op jit(solution)/shard_map/all_to_all | solution.py:286

commit v4 on v3

--- a/solution.py
+++ b/solution.py
@@ -10,9 +10,10 @@
 
 MINOR = (((1,), (1,)), ((), ()))
 MAJOR = (((0,), (0,)), ((), ()))
-LANES = 128
+GROUP = 8
 AHEAD = 4
 EARLY = 2
+PRE = 1
 
 
 def fourier_rows(frame, first, channels):
@@ -42,15 +43,18 @@
     return real, imag
 
 
-def frame_products(frames, taps, volts_ref, table, held, sems, block, prepare, emit):
+def frame_products(
+    frames, taps, volts_ref, table, held, sems, block, prepare, emit, ready=None, spare=(),
+):
     rows = table.shape[0] // taps
     inputs = volts_ref.shape[1]
     count = len(frames)
+    have = 0 if ready is None else ready.shape[0]
     unit = block
     per = 1
     copies = []
     for start in range(0, inputs, block):
-        for k in range(count):
+        for k in range(have, count):
             for at in range(start, start + block, unit):
                 place = len(copies)
                 copies.append(
@@ -60,6 +64,7 @@
                         sems.at[place],
                     )
                 )
+    copies += spare
     for copy in copies[:EARLY]:
         copy.start()
     prepare()
@@ -69,14 +74,16 @@
     for start in range(0, inputs, block):
         sums = {}
         for k in range(count):
-            for copy in copies[done : done + per]:
-                copy.wait()
-            for copy in copies[done + AHEAD : done + AHEAD + per]:
-                copy.start()
-            done += per
+            if k >= have:
+                for copy in copies[done : done + per]:
+                    copy.wait()
+                for copy in copies[done + AHEAD : done + AHEAD + per]:
+                    copy.start()
+                done += per
+            volts = ready if k < have else held
             terms = lax.dot_general(
                 table[...],
-                held[k, start : start + block],
+                volts[k, start : start + block],
                 MINOR,
                 preferred_element_type=jnp.float32,
             )
@@ -85,11 +92,15 @@
                 at = frames[k] + m
                 sums[at] = sums[at] + part if at in sums else part
         emit(slice(start, start + block), sums)
+    for copy in copies[done + AHEAD :]:
+        copy.start()
+    for copy in copies[done:]:
+        copy.wait()
 
 
 def last_frames_kernel(
-    first, total, taps, block, volts_ref, fir_hbm, own_ref, tail_ref, table, held, sems,
-    fir, loaded,
+    first, total, taps, block, volts_ref, fir_hbm, own_ref, tail_ref, table, next_ref, held, sems,
+    fir, loaded, spared,
 ):
     lag = taps - 1
     rows, frame = table.shape[0] // taps, table.shape[1]
@@ -114,11 +125,22 @@
             own_ref[k, :, at] = sums[total - lag + k]
             tail_ref[k, :, at] = sums[total + k].astype(tail_ref.dtype)
 
+    spare = [
+        pltpu.make_async_copy(
+            volts_ref.at[k, pl.ds(at, block)], next_ref.at[k, pl.ds(at, block)], spared.at[k, i]
+        )
+        for i, at in enumerate(range(0, volts_ref.shape[1], block))
+        for k in range(next_ref.shape[0])
+    ]
     frames = list(range(total - lag, total))
-    frame_products(frames, taps, volts_ref, table, held, sems, block, prepare, emit)
-
-
-def first_frames_kernel(total, taps, block, volts_ref, table_ref, own_ref, sum_ref, held, sems):
+    frame_products(
+        frames, taps, volts_ref, table, held, sems, block, prepare, emit, spare=spare
+    )
+
+
+def first_frames_kernel(
+    total, taps, block, volts_ref, table_ref, own_ref, ready_ref, sum_ref, held, sems
+):
     lag = taps - 1
 
     def emit(at, sums):
@@ -129,28 +151,37 @@
             sum_ref[t, :, at] = value
 
     frames = list(range(total - lag))
-    frame_products(frames, taps, volts_ref, table_ref, held, sems, block, lambda: None, emit)
-
-
-def join_kernel(sum_ref, carried_ref, out_hbm, rows, out, sems):
+    frame_products(
+        frames, taps, volts_ref, table_ref, held, sems, block, lambda: None, emit, ready_ref
+    )
+
+
+def join_kernel(sum_ref, carried_ref, out_hbm, out, sems):
     total, count = sum_ref.shape[0], sum_ref.shape[1] // 2
     lag = carried_ref.shape[0]
-    per = rows.shape[0] // sems.shape[0]
+    size = 2 * total * GROUP
+    shape = (size, size)
+    row = lax.broadcasted_iota(jnp.int32, shape, 0)
+    col = lax.broadcasted_iota(jnp.int32, shape, 1)
+    within = lax.rem(row, 2 * total)
+    part, frame = lax.div(within, total), lax.rem(within, total)
+    source = (2 * frame + part) * GROUP + lax.div(row, 2 * total)
+    move = (source == col).astype(out.dtype)
     copies = []
-    for j in range(rows.shape[0]):
-        at = slice(j * LANES, (j + 1) * LANES)
+    for first in range(0, count, GROUP):
+        pieces = []
         for t in range(total):
-            value = sum_ref[t, :, at]
-            if t < lag:
-                value = value + carried_ref[t, :, at].astype(jnp.float32)
-            for part in range(2):
-                spot = pl.ds(part * total + t, count, stride=2 * total)
-                rows[j, spot, :] = value[part * count : (part + 1) * count]
-        out[:, at] = rows[j].astype(out.dtype)
-        if (j + 1) % per == 0:
-            at = slice((j + 1 - per) * LANES, (j + 1) * LANES)
-            copies.append(pltpu.make_async_copy(out.at[:, at], out_hbm.at[:, at], sems.at[j // per]))
-            copies[-1].start()
+            for p in range(2):
+                at = slice(p * count + first, p * count + first + GROUP)
+                value = sum_ref[t, at, :]
+                if t < lag:
+                    value = value + carried_ref[t, at, :].astype(jnp.float32)
+                pieces.append(value)
+        group = jnp.concatenate(pieces, axis=0).astype(out.dtype)
+        at = slice(2 * total * first, 2 * total * first + size)
+        out[at, :] = jnp.dot(move, group, preferred_element_type=jnp.float32).astype(out.dtype)
+        copies.append(pltpu.make_async_copy(out.at[at], out_hbm.at[at], sems.at[len(copies)]))
+        copies[-1].start()
     for copy in copies:
         copy.wait()
 
@@ -246,7 +277,7 @@
         )(*operands)
 
     keep = lambda x: pltpu.with_memory_space_constraint(x, pltpu.HBM)
-    own, tail, table = call(
+    own, tail, table, ready = call(
         functools.partial(last_frames_kernel, first),
         lag,
         (voltages, keep(fir_taps)),
@@ -255,31 +286,31 @@
             jax.ShapeDtypeStruct((lag, rows, inputs_here), jnp.float32),
             jax.ShapeDtypeStruct((lag, rows, inputs_here), jnp.bfloat16),
             jax.ShapeDtypeStruct((taps * rows, frame), jnp.bfloat16),
+            jax.ShapeDtypeStruct((PRE, inputs_here, frame), voltages.dtype),
         ],
         [
             pltpu.VMEM(fir_taps.shape, fir_taps.dtype),
             pltpu.SemaphoreType.DMA,
+            pltpu.SemaphoreType.DMA((PRE, inputs_here // block)),
         ],
     )
     carried = lax.ppermute(tail, "section", [(i, i + 1) for i in range(section_count - 1)])
     (sums,) = call(
         first_frames_kernel,
         spec_dev - lag,
-        (voltages, table, own),
-        [stay, whole, whole],
+        (voltages, table, own, ready),
+        [stay, whole, whole, whole],
         [jax.ShapeDtypeStruct((spec_dev, rows, inputs_here), jnp.float32)],
         [],
     )
-    lane_blocks = inputs_here // LANES
     spectra = pl.pallas_call(
         join_kernel,
         in_specs=[whole] * 2,
         out_specs=pl.BlockSpec(memory_space=pl.ANY),
         out_shape=jax.ShapeDtypeStruct((rows * spec_dev, inputs_here), jnp.bfloat16),
         scratch_shapes=[
-            pltpu.VMEM((lane_blocks, rows * spec_dev, LANES), jnp.float32),
             pltpu.VMEM((rows * spec_dev, inputs_here), jnp.bfloat16),
-            pltpu.SemaphoreType.DMA((min(4, lane_blocks),)),
+            pltpu.SemaphoreType.DMA((channels // GROUP,)),
         ],
         compiler_params=pltpu.CompilerParams(vmem_limit_bytes=12 << 20),
     )(sums, carried)

time: 61 us -> 59.5 us (0.975)
  Pallas kernels: 24.1 us -> 22.7 us
    pallas_call x1, Pallas kernels: 1.94 us -> 1.22 us  [on_device(): pl.pallas_call(join_kernel, in_specs=[whole] * 2, out_specs=pl.BlockSpec(...]
    pallas_call x2, Pallas kernels: 14.9 us -> 14.2 us  [call(): pl.pallas_call(functools.partial(kernel, spec_dev, taps, block), in_specs...]
  transfers between devices with their start and end apart: 2 -> 2, of which waited for: 1 -> 1; matrix products, arithmetic and copies ran while one was open for 2% -> 2% of each run, Pallas kernels for 14% -> 13%
where the time goes in v4:
time: 59.5 us; the launch traced here: 59.3 us
  waiting for transfers between devices  25 us (42%)
  Pallas kernels  22.7 us (38%)
  starting transfers between devices  9.67 us (16%)
  other arithmetic  1.01 us (2%)
  between operations  0.89 us (1%)
    all_to_all x1, waiting for transfers between devices, on_device(): lax.all_to_all(spectra.reshape(devices, 2 * spec_dev, inputs_here), ('sec...  25 us
    pallas_call x2, Pallas kernels, call(): pl.pallas_call(functools.partial(kernel, spec_dev, taps, block), in_specs...  14.2 us
    pallas_call x1, Pallas kernels, on_device(): pl.pallas_call(functools.partial(channel_kernel, 1.0 / math.sqrt(total_fr...  7.3 us
    all_to_all x1, starting transfers between devices, on_device(): lax.all_to_all(spectra.reshape(devices, 2 * spec_dev, inputs_here), ('sec...  7.29 us
    ppermute x1, starting transfers between devices, on_device(): lax.ppermute(tail, 'section', [(i, i + 1) for i in range(section_count -...  2.38 us
    pallas_call x1, Pallas kernels, on_device(): pl.pallas_call(join_kernel, in_specs=[whole] * 2, out_specs=pl.BlockSpec(...  1.22 us
  transfers between devices with their start and end apart: 2, of which 1 were waited for; matrix products, arithmetic and copies ran while one was open for 2% of the time, Pallas kernels for 13%

profile of v4, /device:TPU:0, one launch (start us, length us, event | category | flops | bytes accessed | tf_op | source)
XLA Modules:
  0.0 59.3 jit_solution(8721720015308229289)
XLA Ops:
  0.6 6.3 %shard_map.68 = (f32[3,64,1024]{2,1,0:T(8,128)S(1)}, bf16[3,64,1024]{2,1,0:T(8,128)(2,1)S(1)}, bf16[256,2048]{1,0:T(8,128)(2,1)S(1)}, bf16[1,1024,2048]{2,1,0:T(8,128)(2,1)S(1)}) custom-call(bf16[8,1024,2048]{2,1,0:T(8,128)(2,1)} %volts_ref.3, f32[4,2048]{1,0:T(4,128)} %fir_hbm.1), custom_call_target="tpu_custom_call" | custom-call | flops 3221225472 | bytes 12582912 | tf_op jit(solution)/shard_map/pallas_call | solution.py:261
  6.9 2.4 %collective-permute-start = (bf16[3,64,1024]{2,1,0:T(8,128)(2,1)S(1)}, bf16[3,64,1024]{2,1,0:T(8,128)(2,1)S(1)}, u32[]{:S(2)}, u32[]{:S(2)}) collective-permute-start(bf16[3,64,1024]{2,1,0:T(8,128)(2,1)S(1)} %get-tuple-element.11), channel_id=1, source_target_pairs={{0,2},{2,4},{4,6},{6,8},{8,10},{10,12},{12,14},{14,16},{16,18},{18... | collective-permute-start | bytes 1179656 | tf_op jit(solution)/shard_map/ppermute | solution.py:297
  9.3 0.0 copy-start.2
  9.3 0.0 copy-start
  9.3 0.0 copy-start.1
  9.3 7.9 %shard_map.69.sum_ref = f32[8,64,1024]{2,1,0:T(8,128)S(1)} custom-call(bf16[8,1024,2048]{2,1,0:T(8,128)(2,1)} %volts_ref.3, bf16[256,2048]{1,0:T(8,128)(2,1)S(1)} %get-tuple-element.8.table_ref, f32[3,64,1024]{2,1,0:T(8,128)S(1)} %get-tuple-element.9.own_ref, bf16[1,1024,2048]{2,1,0:T(8,128)(2,1)S(1)} %get-tuple-element.10.ready_ref), custom_call_target="tpu_custom_call" | custom-call | flops 5368709120 | bytes 20971520 | tf_op jit(solution)/shard_map/pallas_call | solution.py:261
  17.3 0.0 collective-permute-done.carried_ref
  17.3 1.2 %shard_map.70 = bf16[512,1024]{1,0:T(8,128)(2,1)} custom-call(f32[8,64,1024]{2,1,0:T(8,128)S(1)} %shard_map.69.sum_ref, bf16[3,64,1024]{2,1,0:T(8,128)(2,1)S(1)} %collective-permute-done.carried_ref), custom_call_target="tpu_custom_call" | custom-call | tf_op jit(solution)/shard_map/pallas_call | solution.py:306
  18.5 7.3 %all-to-all-start = ((bf16[32,16,1024]{2,1,0:T(8,128)(2,1)}), bf16[32,16,1024]{2,1,0:T(8,128)(2,1)S(1)}, u32[]{:S(2)}, u32[]{:S(2)}) async-start(bf16[32,16,1024]{2,1,0:T(8,128)(2,1)} %bitcast), calls=%async_computation | async-start | bytes 2097152 | tf_op jit(solution)/shard_map/all_to_all | solution.py:317
  25.8 0.0 copy-done.2
  25.8 1.0 %multiply_convert_fusion.1 = (bf16[32,2048]{1,0:T(8,128)(2,1)S(1)}, bf16[32,2048]{1,0:T(8,128)(2,1)S(1)}) fusion(f32[32,2048]{1,0:T(8,128)S(1)} %copy-done.2, f32[]{:T(128)S(6)} %convert_element_type.4), kind=kLoop, calls=%fused_computation.2 | loop fusion | flops 393216 | bytes 524292 | tf_op jit(solution)/shard_map/convert
  26.8 25.0 %all-to-all-done = bf16[32,16,1024]{2,1,0:T(8,128)(2,1)S(1)} async-done(((bf16[32,16,1024]{2,1,0:T(8,128)(2,1)}), bf16[32,16,1024]{2,1,0:T(8,128)(2,1)S(1)}, u32[]{:S(2)}, u32[]{:S(2)}) %all-to-all-start) | async-done | bytes 1048608 | tf_op jit(solution)/shard_map/all_to_all | solution.py:317
  51.9 0.0 copy-done
  51.9 0.0 copy-done.1
  51.9 7.3 %shard_map.71 = (bf16[2048,2048]{1,0:T(8,128)(2,1)}, bf16[2,1024,128]{2,1,0:T(8,128)(2,1)}) custom-call(bf16[16,2,16,1024]{3,2,1,0:T(8,128)(2,1)S(1)} %bitcast.6, s32[1,2048]{1,0:T(1,128)S(1)} %bitcast.7, bf16[64,2048]{1,0:T(8,128)(2,1)S(1)} %pad_maximum_fusion.weight_ref, s32[1,1024]{1,0:T(1,128)S(1)} %bitcast.8), custom_call_target="tpu_custom_call" | custom-call | tf_op jit(solution)/shard_map/pallas_call | solution.py:334
  (1 shorter events, 0.0 us)
Async XLA Ops:
  6.9 10.3 %collective-permute-start = (bf16[3,64,1024]{2,1,0:T(8,128)(2,1)S(1)}, bf16[3,64,1024]{2,1,0:T(8,128)(2,1)S(1)}, u32[]{:S(2)}, u32[]{:S(2)}) collective-permute-start(bf16[3,64,1024]{2,1,0:T(8,128)(2,1)S(1)} %get-tuple-element.11), channel_id=1, source_target_pairs={{0,2},{2,4},{4,6},{6,8},{8,10},{10,12},{12,14},{14,16},{16,18},{18... | collective-permute-start | bytes 1179656 | tf_op jit(solution)/shard_map/ppermute | solution.py:297
  9.3 16.5 %copy-start.2 = (f32[32,2048]{1,0:T(8,128)S(1)}, f32[32,2048]{1,0:T(8,128)}, u32[]{:S(2)}) copy-start(f32[32,2048]{1,0:T(8,128)} %param.7) | copy-start | bytes 786436
  9.3 42.5 %copy-start = (s32[2048]{0:T(1024)S(1)}, s32[2048]{0:T(1024)}, u32[]{:S(2)}) copy-start(s32[2048]{0:T(1024)} %param.9) | copy-start | bytes 24580
  9.3 42.5 %copy-start.1 = (s32[1024]{0:T(1024)S(1)}, s32[1024]{0:T(1024)}, u32[]{:S(2)}) copy-start(s32[1024]{0:T(1024)} %param.8) | copy-start | bytes 12292
  18.5 33.4 %all-to-all-start = ((bf16[32,16,1024]{2,1,0:T(8,128)(2,1)}), bf16[32,16,1024]{2,1,0:T(8,128)(2,1)S(1)}, u32[]{:S(2)}, u32[]{:S(2)}) async-start(bf16[32,16,1024]{2,1,0:T(8,128)(2,1)} %bitcast), calls=%async_computation | async-start | bytes 2097152 | tf_op jit(solution)/shard_map/all_to_all | solution.py:317
